TPU v7x, 32 devices: a whole 2x2x4 slice. The times are simulated.
32 devices in a mesh: groups: 2 (over y), tiles: 4 (over z), rhs: 2 (over x), sub: 2 (over core).
Axes of the slice: x: 2, y: 2, z: 4, core: 2. Of those that a mesh axis runs over, the one named last changes fastest.
Arguments:
- sources: bfloat16 [256, 8192], P('rhs', ('groups', 'tiles', 'sub')), parts along dimension 1, may hold values from -6 to 6
- basis_out: bfloat16 [384, 64, 512], P(('groups', 'tiles', 'rhs', 'sub')), parts along dimension 0, may hold values from -0.15625 to 0.15625
- basis_in: bfloat16 [384, 64, 512], P(('groups', 'tiles', 'rhs', 'sub')), parts along dimension 0, may hold values from -0.25 to 0.25
- tile_rank: int32 [384], P(('groups', 'tiles', 'rhs', 'sub')), parts along dimension 0, may hold values from 1 to 64, as said below
- tile_row: int32 [384], P(('groups', 'tiles', 'rhs', 'sub')), parts along dimension 0, may hold values from 0 to 7
- tile_col: int32 [384], P(('groups', 'tiles', 'rhs', 'sub')), parts along dimension 0, may hold values from 0 to 7
- near_blocks: bfloat16 [16, 16, 512, 512], P(('groups', 'tiles', 'sub')), parts along dimension 0, may hold values from -0.0625 to 0.0625
- near_col: int32 [16, 16], P(('groups', 'tiles', 'sub')), parts along dimension 0, may hold values from 0 to 7
- jacobi_inverse: bfloat16 [64, 128, 128], P(('groups', 'tiles', 'sub')), parts along dimension 0
Outputs:
- first_result: bfloat16 [256, 8192], P('rhs', ('groups', 'tiles', 'sub')), parts along dimension 1
- second_result: bfloat16 [256, 8192], P('rhs', ('groups', 'tiles', 'sub')), parts along dimension 1
There are 2 independent parts, one for each index of `groups`. A program takes and returns all parts, laid end to end along the dimension named above; each array names one. Nothing has to cross between parts.
Inputs may be any that keep to these rules, and one draw needn't show every extreme that they name: `tile_rank`: every rank lies in 1 to 64, and some tile has rank 64.
All inputs are finite; a program needn't handle non-finite values.
Results may differ from a plain program's by a relative error of at most 0.03.
Values may be sent and summed in bfloat16 or wider, within the bound.
No kernel may reach another device: no remote copies, remote signals or barrier semaphores. Data moves between devices by JAX's collectives and lax.ppermute only.
A program may use at most 128 MiB of HBM per device.

v0:
```python
import jax
import jax.numpy as jnp
from jax import lax
from jax.sharding import PartitionSpec as P

BLK = 512
RMAX = 64
JB = 128


def tile_terms(running, pieces, gathered):
    basis_out, basis_in, tile_rank, tile_row, tile_col = pieces
    picked = jnp.take(gathered, tile_col, axis=1)
    coefficients = jnp.einsum("ctq,trq->ctr", picked, basis_in, preferred_element_type=jnp.float32)
    rank_iota = lax.broadcasted_iota(jnp.int32, (1, tile_rank.shape[0], RMAX), 2)
    kept_mask = rank_iota < tile_rank[None, :, None]
    coefficients = jnp.where(kept_mask, coefficients, jnp.zeros_like(coefficients)).astype(
        jnp.bfloat16
    )
    contrib = jnp.einsum(
        "ctr,trp->ctp", coefficients, basis_out, preferred_element_type=jnp.float32
    )
    upper = contrib.astype(jnp.bfloat16)
    lower = (contrib - upper.astype(jnp.float32)).astype(jnp.bfloat16)
    block_iota = lax.broadcasted_iota(jnp.int32, (1, running.shape[1]), 1)
    onehot = (tile_row[:, None] == block_iota).astype(jnp.bfloat16)
    placed_upper = jnp.einsum("ctp,tb->cbp", upper, onehot, preferred_element_type=jnp.float32)
    placed_lower = jnp.einsum("ctp,tb->cbp", lower, onehot, preferred_element_type=jnp.float32)
    return placed_upper + placed_lower


def apply_operator(vector, tile_apply, near_blocks, near_col):
    columns = vector.shape[0]
    gathered = lax.all_gather(vector, ("tiles", "sub"), axis=1, tiled=True).reshape(
        columns, -1, BLK
    )
    zero_sums = jnp.zeros(gathered.shape, jnp.float32)
    far_field = tile_apply(zero_sums, gathered).reshape(columns, -1)
    far_field = lax.psum_scatter(
        far_field.astype(jnp.bfloat16), ("tiles", "sub"), scatter_dimension=1, tiled=True
    ).astype(jnp.float32)
    picked = jnp.take(gathered, near_col, axis=1)
    near_field = jnp.einsum(
        "cikq,ikpq->cip", picked, near_blocks, preferred_element_type=jnp.float32
    )
    return (far_field + near_field.reshape(columns, -1)).astype(jnp.bfloat16)


def precondition(field, jacobi_inverse):
    columns = field.shape[0]
    grouped = field.reshape(columns, -1, JB)
    result = jnp.einsum("cgq,gpq->cgp", grouped, jacobi_inverse, preferred_element_type=jnp.float32)
    return result.astype(jnp.bfloat16).reshape(columns, -1)


def local(
    sources,
    basis_out,
    basis_in,
    tile_rank,
    tile_row,
    tile_col,
    near_blocks,
    near_col,
    jacobi_inverse,
):

    def tile_apply(running, gathered):
        return tile_terms(
            running,
            (
                lax.all_gather(basis_out, "rhs", axis=0, tiled=True),
                lax.all_gather(basis_in, "rhs", axis=0, tiled=True),
                lax.all_gather(tile_rank, "rhs", axis=0, tiled=True),
                lax.all_gather(tile_row, "rhs", axis=0, tiled=True),
                lax.all_gather(tile_col, "rhs", axis=0, tiled=True),
            ),
            gathered,
        )

    first_result = precondition(
        apply_operator(sources, tile_apply, near_blocks, near_col), jacobi_inverse
    )
    second_result = precondition(
        apply_operator(first_result, tile_apply, near_blocks, near_col), jacobi_inverse
    )
    return (first_result, second_result)


def solution(mesh):
    return jax.shard_map(
        local,
        mesh=mesh,
        in_specs=(
            P("rhs", ("groups", "tiles", "sub")),
            P(("groups", "tiles", "rhs", "sub"), None, None),
            P(("groups", "tiles", "rhs", "sub"), None, None),
            P(("groups", "tiles", "rhs", "sub")),
            P(("groups", "tiles", "rhs", "sub")),
            P(("groups", "tiles", "rhs", "sub")),
            P(("groups", "tiles", "sub"), None, None, None),
            P(("groups", "tiles", "sub"), None),
            P(("groups", "tiles", "sub"), None, None),
        ),
        out_specs=(P("rhs", ("groups", "tiles", "sub")), P("rhs", ("groups", "tiles", "sub"))),
        check_vma=False,
    )
```

profile of v0, /device:TPU:0, one launch (start us, length us, event | category | flops | bytes accessed | tf_op | source)
XLA Modules:
  0.0 233.3 jit_solution(618950563438700425)
XLA Ops:
  7.2 0.0 copy-start
  7.2 0.0 all-gather.5.cloned.1.call-start
  7.2 1.7 copy.40
  8.9 0.0 all-gather.5.cloned.1.call-update
  8.9 0.0 all-gather.7.cloned.1.call-start
  9.0 0.7 all-gather.7.cloned.1.call-update
  9.7 0.0 all-gather.9.cloned.1.call-start
  9.7 0.7 all-gather.9.cloned.1.call-update
  10.4 0.0 reduce-scatter.3.cloned.1.call-start
  10.5 1.2 dynamic-slice
  12.4 0.9 dynamic-update-slice
  13.2 0.8 dynamic-update-slice.1
  14.1 0.8 dynamic-update-slice.2
  14.9 5.2 %all-reduce.3 = (s32[24]{0:T(128)S(1)}, s32[24]{0:T(128)S(1)}, s32[24]{0:T(128)S(1)}) all-reduce(s32[24]{0:T(128)S(1)} %dynamic-update-slice.2, s32[24]{0:T(128)S(1)} %dynamic-update-slice.1, s32[24]{0:T(128)S(1)} %dynamic-update-slice), channel_id=1, replica_groups=mesh['groups'=2,'tiles'=4,'rhs'=2,'sub'=2] {'rhs'}, use_global_device_ids=true, to_apply=%add.2 | all-reduce | flops 72 | bytes 576
  20.1 0.1 iota_compare_fusion
  20.2 14.8 %all-gather.5.cloned.1.call-done = bf16[128,4096]{0,1:T(8,128)(2,1)} async-done(((bf16[128,512]{0,1:T(8,128)(2,1)}), bf16[128,4096]{0,1:T(8,128)(2,1)}) %all-gather.5.cloned.1.call-update) | async-done | bytes 1048592 | tf_op jit(solution)/shard_map/all_gather | solution.py:34
  35.0 1.5 copy.41
  36.5 2.5 %gather_fusion = bf16[24,128,512]{2,1,0:T(8,128)(2,1)} fusion(bf16[128,8,512]{2,0,1:T(8,128)(2,1)S(1)} %copy.41, s32[1024]{0:T(1024)S(1)} %pad_clamp_fusion.1), kind=kCustom, calls=%fused_computation.clone | custom fusion | bytes 6291552 | tf_op jit(solution)/shard_map/jit(_take)/gather | solution.py:13
  39.0 24.4 %all-gather.7.cloned.1.call-done = bf16[24,64,512]{2,1,0:T(8,128)(2,1)} async-done(((bf16[12,64,512]{2,1,0:T(8,128)(2,1)}), bf16[24,64,512]{2,1,0:T(8,128)(2,1)}) %all-gather.7.cloned.1.call-update) | async-done | bytes 1572880 | tf_op jit(solution)/shard_map/all_gather | solution.py:73
  63.4 28.8 %all-gather.9.cloned.1.call-done = bf16[24,64,512]{2,1,0:T(8,128)(2,1)} async-done(((bf16[12,64,512]{2,1,0:T(8,128)(2,1)}), bf16[24,64,512]{2,1,0:T(8,128)(2,1)}) %all-gather.9.cloned.1.call-update) | async-done | bytes 1572880 | tf_op jit(solution)/shard_map/all_gather | solution.py:72
  92.2 7.7 %fusion.5 = (bf16[128,24,512]{2,0,1:T(8,128)(2,1)}, bf16[128,24,512]{2,0,1:T(8,128)(2,1)}) fusion(bf16[24,64,512]{2,1,0:T(8,128)(2,1)} %all-gather.9.cloned.1.call-done, bf16[24,64,512]{2,1,0:T(8,128)(2,1)} %all-gather.7.cloned.1.call-done, bf16[24,128,512]{2,1,0:T(8,128)(2,1)} %gather_fusion, pred[24]{0:T(512)(128)(4,1)S(1)} %compare_and_fusion, ...), kind=kOutput, calls=%fused_computation.13 | convolution fusion | flops 410910720 | bytes 12584472 | tf_op jit(solution)/shard_map/ctr,trp->ctp/dot_general | solution.py:20
  100.0 4.3 %fusion.14 = f32[8,128,512]{2,0,1:T(8,128)S(1)} fusion(bf16[128,24,512]{2,0,1:T(8,128)(2,1)} %get-tuple-element.17, s32[24]{0:T(128)S(1)} %get-tuple-element.14), kind=kOutput, calls=%fused_computation.22 | convolution fusion | flops 25166016 | bytes 5242976 | tf_op jit(solution)/shard_map/ctp,tb->cbp/dot_general | solution.py:28
  104.2 0.0 copy-done.2
  104.2 2.3 add_convert_fusion.1
  106.5 1.4 copy.56
  107.9 0.0 reduce-scatter.3.cloned.1.call-update
  107.9 0.0 all-gather.11.cloned.1.call-start
  108.0 0.0 copy-done.4
  108.0 0.7 gather_fusion.1
  108.7 31.8 %reduce-scatter.3.cloned.1.call-done = bf16[128,512]{1,0:T(8,128)(2,1)} async-done(((bf16[128,4096]{1,0:T(8,128)(2,1)}), bf16[128,512]{1,0:T(8,128)(2,1)}) %reduce-scatter.3.cloned.1.call-update) | async-done | bytes 131088 | tf_op jit(solution)/shard_map/reduce_scatter | solution.py:39
  140.6 6.2 %fusion.93 = bf16[16,4,8,128]{3,2,1,0:T(8,128)(2,1)S(1)} fusion(bf16[1,16,512,512]{3,2,1,0:T(8,128)(2,1)} %param.19, bf16[16,128,512]{2,1,0:T(8,128)(2,1)S(1)} %gather_fusion.1, pred[16]{0:T(512)(128)(4,1)S(1)} %and_bitcast_fusion, bf16[128,512]{1,0:T(8,128)(2,1)} %reduce-scatter.3.cloned.1.call-done), kind=kOutput, calls=%fused_computation.57 | convolution fusion | flops 1074987008 | bytes 10747920 | tf_op jit(solution)/shard_map/cikq,ikpq->cip/dot_general | solution.py:43
  146.8 0.9 convolution_convert_fusion.1
  147.7 0.0 all-gather.11.cloned.1.call-update
  147.7 0.2 reduce-scatter.5.cloned.1.call-start
  147.9 20.2 %all-gather.11.cloned.1.call-done = bf16[128,4096]{0,1:T(8,128)(2,1)} async-done(((bf16[128,512]{0,1:T(8,128)(2,1)}), bf16[128,4096]{0,1:T(8,128)(2,1)}) %all-gather.11.cloned.1.call-update) | async-done | bytes 1048592 | tf_op jit(solution)/shard_map/all_gather | solution.py:34
  168.1 3.9 %gather_fusion.2 = bf16[24,128,512]{1,2,0:T(8,128)(2,1)} fusion(bf16[128,8,512]{0,2,1:T(8,128)(2,1)} %bitcast.182, s32[1024]{0:T(1024)S(1)} %pad_clamp_fusion.1), kind=kCustom, calls=%fused_computation.2.clone | custom fusion | bytes 6291552 | tf_op jit(solution)/shard_map/jit(_take)/gather | solution.py:13
  172.0 6.7 %fusion.4 = (bf16[128,24,512]{2,0,1:T(8,128)(2,1)}, bf16[128,24,512]{2,0,1:T(8,128)(2,1)S(1)}) fusion(bf16[24,64,512]{2,1,0:T(8,128)(2,1)} %all-gather.9.cloned.1.call-done, bf16[24,64,512]{2,1,0:T(8,128)(2,1)} %all-gather.7.cloned.1.call-done, bf16[24,128,512]{1,2,0:T(8,128)(2,1)} %gather_fusion.2, pred[24]{0:T(512)(128)(4,1)S(1)} %compare_and_fusion, ...), kind=kOutput, calls=%fused_computation.10 | convolution fusion | flops 410910720 | bytes 12584472 | tf_op jit(solution)/shard_map/ctr,trp->ctp/dot_general | solution.py:20
  178.7 4.1 %fusion.10 = f32[8,128,512]{2,0,1:T(8,128)S(1)} fusion(bf16[128,24,512]{2,0,1:T(8,128)(2,1)} %get-tuple-element.15, s32[24]{0:T(128)S(1)} %get-tuple-element.14), kind=kOutput, calls=%fused_computation.18 | convolution fusion | flops 25166016 | bytes 5242976 | tf_op jit(solution)/shard_map/ctp,tb->cbp/dot_general | solution.py:28
  182.8 2.3 add_convert_fusion
  185.2 1.4 copy.57
  186.5 0.0 reduce-scatter.5.cloned.1.call-update
  186.5 0.8 copy.51
  187.3 0.5 copy.49
  187.8 2.0 gather_fusion.3
  189.9 28.8 %reduce-scatter.5.cloned.1.call-done = bf16[128,512]{1,0:T(8,128)(2,1)} async-done(((bf16[128,4096]{1,0:T(8,128)(2,1)}), bf16[128,512]{1,0:T(8,128)(2,1)}) %reduce-scatter.5.cloned.1.call-update) | async-done | bytes 131088 | tf_op jit(solution)/shard_map/reduce_scatter | solution.py:39
  218.7 6.8 %fusion.88 = bf16[16,4,8,128]{3,2,1,0:T(8,128)(2,1)S(1)} fusion(bf16[1,16,512,512]{3,2,1,0:T(8,128)(2,1)} %param.19, bf16[16,128,512]{2,1,0:T(8,128)(2,1)} %gather_fusion.3, pred[16]{0:T(512)(128)(4,1)S(1)} %and_bitcast_fusion, bf16[128,512]{1,0:T(8,128)(2,1)} %reduce-scatter.5.cloned.1.call-done), kind=kOutput, calls=%fused_computation.56 | convolution fusion | flops 1074987008 | bytes 10747920 | tf_op jit(solution)/shard_map/cikq,ikpq->cip/dot_general | solution.py:43
  225.5 0.2 convolution_convert_fusion
  225.7 0.8 copy.52
  (16 shorter events, 0.1 us)
Async XLA Ops:
  7.2 139.6 %copy-start = (bf16[4,128,128]{2,1,0:T(8,128)(2,1)S(1)}, bf16[4,128,128]{2,1,0:T(8,128)(2,1)}, u32[]{:S(2)}) copy-start(bf16[4,128,128]{2,1,0:T(8,128)(2,1)} %param.21) | copy-start | bytes 393220
  7.2 27.8 %all-gather.5.cloned.1.call-start = ((), (), s32[]{:S(2)}) async-start(), calls=%async_computation.2 | async-start | bytes 1179648 | tf_op jit(solution)/shard_map/all_gather | solution.py:34
  8.9 54.5 %all-gather.7.cloned.1.call-start = ((), (), s32[]{:S(2)}) async-start(), calls=%async_computation.3 | async-start | bytes 2359296 | tf_op jit(solution)/shard_map/all_gather | solution.py:73
  9.7 82.5 %all-gather.9.cloned.1.call-start = ((), (), s32[]{:S(2)}) async-start(), calls=%async_computation.4 | async-start | bytes 2359296 | tf_op jit(solution)/shard_map/all_gather | solution.py:72
  10.4 130.1 %reduce-scatter.3.cloned.1.call-start = ((), (), s32[]{:S(2)}) async-start(), calls=%async_computation.5 | async-start | bytes 1179648 | tf_op jit(solution)/shard_map/reduce_scatter | solution.py:39
  100.0 4.3 %copy-start.2 = (bf16[128,24,512]{2,0,1:T(8,128)(2,1)S(1)}, bf16[128,24,512]{2,0,1:T(8,128)(2,1)}, u32[]{:S(2)}) copy-start(bf16[128,24,512]{2,0,1:T(8,128)(2,1)} %get-tuple-element.18) | copy-start | bytes 9437188
  106.5 1.5 copy-start.4
  107.9 60.2 %all-gather.11.cloned.1.call-start = ((), (), s32[]{:S(2)}) async-start(), calls=%async_computation.6 | async-start | bytes 1179648 | tf_op jit(solution)/shard_map/all_gather | solution.py:34
  147.7 71.0 %reduce-scatter.5.cloned.1.call-start = ((), (), s32[]{:S(2)}) async-start(), calls=%async_computation.7 | async-start | bytes 1179648 | tf_op jit(solution)/shard_map/reduce_scatter | solution.py:39
  185.1 1.4 copy-start.3
  185.1 2.2 copy-start.1
Sparse Core Ops, SparseCore 0:
  10.2 24.7 all-gather.4
  36.6 26.8 all-gather.6
  65.0 27.1 all-gather.8
  108.0 32.4 reduce-scatter.2
  147.8 20.2 all-gather.10
  186.7 31.9 reduce-scatter.4
where the time goes:
time: 234 us; the launch traced here: 233 us
  waiting for transfers between devices  150 us (64%)
  matrix products  41.5 us (18%)
  local copies, waits for them, and re-layouts  20.9 us (9%)
  between operations  14.9 us (6%)
  blocking collectives  5.19 us (2%)
    reduce_scatter x2, waiting for transfers between devices, apply_operator(): lax.psum_scatter(far_field.astype(jnp.bfloat16), ('tiles', 'sub'), scatte...  60.7 us
    all_gather x2, waiting for transfers between devices, apply_operator(): lax.all_gather(vector, ('tiles', 'sub'), axis=1, tiled=True)  35 us
    all_gather x1, waiting for transfers between devices, tile_apply(): lax.all_gather(basis_out, 'rhs', axis=0, tiled=True)  28.8 us
    all_gather x1, waiting for transfers between devices, tile_apply(): lax.all_gather(basis_in, 'rhs', axis=0, tiled=True)  24.4 us
    dot_general x2, matrix products, tile_terms(): jnp.einsum('ctr,trp->ctp', coefficients, basis_out, preferred_element_typ...  14.4 us
    dot_general x2, matrix products, apply_operator(): jnp.einsum('cikq,ikpq->cip', picked, near_blocks, preferred_element_type=...  13 us
    unnamed x22, local copies, waits for them, and re-layouts  9.77 us
    dot_general x2, matrix products, tile_terms(): jnp.einsum('ctp,tb->cbp', lower, onehot, preferred_element_type=jnp.float32)  8.39 us
  transfers between devices with their start and end apart: 6, of which 6 were waited for; matrix products, arithmetic and copies ran while one was open for 5% of the time, Pallas kernels for 0%

commit v1 on v0

--- a/solution.py
+++ b/solution.py
@@ -6,6 +6,18 @@
 BLK = 512
 RMAX = 64
 JB = 128
+
+
+def collect(x, axis, dim):
+    ways, here, step = (lax.axis_size(axis), lax.axis_index(axis), x.shape[dim])
+    line, have = (x, 1)
+    while have < ways:
+        line = jnp.concatenate(
+            [line, lax.ppermute(line, axis, [(d, (d - have) % ways) for d in range(ways)])],
+            axis=dim,
+        )
+        have = 2 * have
+    return jnp.roll(line, here * step, axis=dim)
 
 
 def tile_terms(running, pieces, gathered):
@@ -70,7 +82,7 @@
             running,
             (
                 lax.all_gather(basis_out, "rhs", axis=0, tiled=True),
-                lax.all_gather(basis_in, "rhs", axis=0, tiled=True),
+                collect(basis_in, "rhs", 0),
                 lax.all_gather(tile_rank, "rhs", axis=0, tiled=True),
                 lax.all_gather(tile_row, "rhs", axis=0, tiled=True),
                 lax.all_gather(tile_col, "rhs", axis=0, tiled=True),

time: 234 us -> 205 us (0.88)
  waiting for transfers between devices: 150 us -> 107 us
  blocking collectives: 5.19 us -> 13.4 us
  starting transfers between devices: 0.42 us -> 3.39 us
    all_gather x1 -> x0, waiting for transfers between devices: 24.4 us -> none  [tile_apply(): lax.all_gather(basis_in, 'rhs', axis=0, tiled=True)]
    all_gather x2, waiting for transfers between devices: 35 us -> 22.5 us  [apply_operator(): lax.all_gather(vector, ('tiles', 'sub'), axis=1, tiled=True)]
    unnamed x1, blocking collectives: 5.19 us -> 13.4 us
    all_gather x1, waiting for transfers between devices: 28.8 us -> 24.3 us  [tile_apply(): lax.all_gather(basis_out, 'rhs', axis=0, tiled=True)]
    ppermute x0 -> x1, starting transfers between devices: none -> 3 us  [collect(): lax.ppermute(line, axis, [(d, (d - have) % ways) for d in range(ways)])]
    unnamed x22 -> x26, local copies, waits for them, and re-layouts: 9.77 us -> 9.75 us
  transfers between devices with their start and end apart: 6 -> 6, of which waited for: 6 -> 5; matrix products, arithmetic and copies ran while one was open for 5% -> 8% of each run, Pallas kernels for 0% -> 0%
where the time goes in v1:
time: 205 us; the launch traced here: 204 us
  waiting for transfers between devices  107 us (52%)
  matrix products  41.7 us (20%)
  local copies, waits for them, and re-layouts  22.3 us (11%)
  between operations  14.6 us (7%)
  blocking collectives  13.4 us (7%)
  starting transfers between devices  3.39 us (2%)
  other arithmetic  2.33 us (1%)
    reduce_scatter x2, waiting for transfers between devices, apply_operator(): lax.psum_scatter(far_field.astype(jnp.bfloat16), ('tiles', 'sub'), scatte...  59.1 us
    all_gather x1, waiting for transfers between devices, tile_apply(): lax.all_gather(basis_out, 'rhs', axis=0, tiled=True)  24.3 us
    all_gather x2, waiting for transfers between devices, apply_operator(): lax.all_gather(vector, ('tiles', 'sub'), axis=1, tiled=True)  22.5 us
    dot_general x2, matrix products, tile_terms(): jnp.einsum('ctr,trp->ctp', coefficients, basis_out, preferred_element_typ...  13.9 us
    dot_general x2, matrix products, apply_operator(): jnp.einsum('cikq,ikpq->cip', picked, near_blocks, preferred_element_type=...  13.6 us
    unnamed x1, blocking collectives  13.4 us
    unnamed x26, local copies, waits for them, and re-layouts  9.75 us
    dot_general x2, matrix products, tile_terms(): jnp.einsum('ctp,tb->cbp', lower, onehot, preferred_element_type=jnp.float32)  8.54 us
  transfers between devices with their start and end apart: 6, of which 5 were waited for; matrix products, arithmetic and copies ran while one was open for 8% of the time, Pallas kernels for 0%

profile of v1, /device:TPU:0, one launch (start us, length us, event | category | flops | bytes accessed | tf_op | source)
XLA Modules:
  0.0 204.4 jit_solution(9321281050885972035)
XLA Ops:
  7.2 0.0 copy-start
  7.2 0.0 all-gather.4.cloned.1.call-start
  7.2 1.7 copy.40
  8.9 0.0 all-gather.4.cloned.1.call-update
  8.9 0.0 all-gather.6.cloned.1.call-start
  9.0 0.7 all-gather.6.cloned.1.call-update
  9.7 0.0 reduce-scatter.3.cloned.1.call-start
  9.7 3.0 %collective-permute-start = (bf16[12,64,512]{2,1,0:T(8,128)(2,1)}, bf16[12,64,512]{2,1,0:T(8,128)(2,1)S(1)}, u32[]{:S(2)}, u32[]{:S(2)}) collective-permute-start(bf16[12,64,512]{2,1,0:T(8,128)(2,1)} %param.17), channel_id=1, source_target_pairs={{0,2},{2,0},{1,3},{3,1},{4,6},{6,4},{5,7},{7,5},{8,10},{10,8},{9,1... | collective-permute-start | bytes 2359304 | tf_op jit(solution)/shard_map/ppermute | solution.py:16
  12.7 1.2 dynamic-slice
  14.6 0.9 dynamic-update-slice
  15.5 0.8 dynamic-update-slice.1
  16.3 0.8 dynamic-update-slice.2
  17.2 13.4 %all-reduce.3 = (s32[24]{0:T(128)S(1)}, s32[24]{0:T(128)S(1)}, s32[24]{0:T(128)S(1)}) all-reduce(s32[24]{0:T(128)S(1)} %dynamic-update-slice.2, s32[24]{0:T(128)S(1)} %dynamic-update-slice.1, s32[24]{0:T(128)S(1)} %dynamic-update-slice), channel_id=1, replica_groups=mesh['groups'=2,'tiles'=4,'rhs'=2,'sub'=2] {'rhs'}, use_global_device_ids=true, to_apply=%add.2 | all-reduce | flops 72 | bytes 576
  30.6 0.1 iota_compare_fusion
  30.7 0.0 collective-permute-done
  30.7 2.2 %fusion.33 = bf16[24,64,512]{2,1,0:T(8,128)(2,1)S(1)} fusion(s32[]{:T(128)S(6)} %select_n.50, bf16[12,64,512]{2,1,0:T(8,128)(2,1)} %param.17, bf16[12,64,512]{2,1,0:T(8,128)(2,1)S(1)} %collective-permute-done), kind=kLoop, calls=%fused_computation.43 | loop fusion | flops 2359296 | bytes 3145732 | tf_op jit(solution)/shard_map/jit(_roll_dynamic)/concatenate | solution.py:20
  32.9 2.1 %all-gather.4.cloned.1.call-done = bf16[128,4096]{0,1:T(8,128)(2,1)} async-done(((bf16[128,512]{0,1:T(8,128)(2,1)}), bf16[128,4096]{0,1:T(8,128)(2,1)}) %all-gather.4.cloned.1.call-update) | async-done | bytes 1048592 | tf_op jit(solution)/shard_map/all_gather | solution.py:46
  35.0 1.5 copy.41
  36.5 2.5 %gather_fusion = bf16[24,128,512]{2,1,0:T(8,128)(2,1)} fusion(bf16[128,8,512]{2,0,1:T(8,128)(2,1)S(1)} %copy.41, s32[1024]{0:T(1024)S(1)} %pad_clamp_fusion.1), kind=kCustom, calls=%fused_computation.clone | custom fusion | bytes 6291552 | tf_op jit(solution)/shard_map/jit(_take)/gather | solution.py:25
  39.0 24.3 %all-gather.6.cloned.1.call-done = bf16[24,64,512]{2,1,0:T(8,128)(2,1)} async-done(((bf16[12,64,512]{2,1,0:T(8,128)(2,1)}), bf16[24,64,512]{2,1,0:T(8,128)(2,1)}) %all-gather.6.cloned.1.call-update) | async-done | bytes 1572880 | tf_op jit(solution)/shard_map/all_gather | solution.py:84
  63.3 7.3 %fusion.5 = (bf16[128,24,512]{2,0,1:T(8,128)(2,1)}, bf16[128,24,512]{2,0,1:T(8,128)(2,1)}) fusion(bf16[24,64,512]{2,1,0:T(8,128)(2,1)} %all-gather.6.cloned.1.call-done, bf16[24,64,512]{2,1,0:T(8,128)(2,1)S(1)} %fusion.33, bf16[24,128,512]{2,1,0:T(8,128)(2,1)} %gather_fusion, pred[24]{0:T(512)(128)(4,1)S(1)} %compare_and_fusion, ...), kind=kOutput, calls=%fused_computation.13 | convolution fusion | flops 410910720 | bytes 12584472 | tf_op jit(solution)/shard_map/ctr,trp->ctp/dot_general | solution.py:32
  70.6 4.3 %fusion.14 = f32[8,128,512]{2,0,1:T(8,128)S(1)} fusion(bf16[128,24,512]{2,0,1:T(8,128)(2,1)} %get-tuple-element.18, s32[24]{0:T(128)S(1)} %get-tuple-element.15), kind=kOutput, calls=%fused_computation.26 | convolution fusion | flops 25166016 | bytes 5242976 | tf_op jit(solution)/shard_map/ctp,tb->cbp/dot_general | solution.py:40
  74.9 0.0 copy-done.3
  74.9 2.3 %add_convert_fusion.1 = bf16[8,128,512]{2,0,1:T(8,128)(2,1)S(1)} fusion(f32[8,128,512]{2,0,1:T(8,128)S(1)} %fusion.14, bf16[128,24,512]{2,0,1:T(8,128)(2,1)S(1)} %copy-done.3, s32[24]{0:T(128)S(1)} %get-tuple-element.15), kind=kOutput, calls=%fused_computation.39 | convolution fusion | flops 26214592 | bytes 6291552 | tf_op jit(solution)/shard_map/ctp,tb->cbp/dot_general | solution.py:39
  77.2 1.4 copy.56
  78.5 0.0 reduce-scatter.3.cloned.1.call-update
  78.5 0.0 all-gather.8.cloned.1.call-start
  78.6 0.0 copy-done.6
  78.6 2.0 gather_fusion.1
  80.7 30.3 %reduce-scatter.3.cloned.1.call-done = bf16[128,512]{1,0:T(8,128)(2,1)} async-done(((bf16[128,4096]{1,0:T(8,128)(2,1)}), bf16[128,512]{1,0:T(8,128)(2,1)}) %reduce-scatter.3.cloned.1.call-update) | async-done | bytes 131088 | tf_op jit(solution)/shard_map/reduce_scatter | solution.py:51
  110.9 6.8 %fusion.96 = bf16[16,4,8,128]{3,2,1,0:T(8,128)(2,1)S(1)} fusion(bf16[1,16,512,512]{3,2,1,0:T(8,128)(2,1)} %param.21, bf16[16,128,512]{2,1,0:T(8,128)(2,1)} %gather_fusion.1, pred[16]{0:T(512)(128)(4,1)S(1)} %and_bitcast_fusion, bf16[128,512]{1,0:T(8,128)(2,1)} %reduce-scatter.3.cloned.1.call-done), kind=kOutput, calls=%fused_computation.64 | convolution fusion | flops 1074987008 | bytes 10747920 | tf_op jit(solution)/shard_map/cikq,ikpq->cip/dot_general | solution.py:55
  117.8 0.9 convolution_convert_fusion.1
  118.6 0.0 all-gather.8.cloned.1.call-update
  118.6 0.2 reduce-scatter.5.cloned.1.call-start
  118.9 20.4 %all-gather.8.cloned.1.call-done = bf16[128,4096]{0,1:T(8,128)(2,1)} async-done(((bf16[128,512]{0,1:T(8,128)(2,1)}), bf16[128,4096]{0,1:T(8,128)(2,1)}) %all-gather.8.cloned.1.call-update) | async-done | bytes 1048592 | tf_op jit(solution)/shard_map/all_gather | solution.py:46
  139.3 4.0 %gather_fusion.2 = bf16[24,128,512]{1,2,0:T(8,128)(2,1)} fusion(bf16[128,8,512]{0,2,1:T(8,128)(2,1)} %bitcast.182, s32[1024]{0:T(1024)S(1)} %pad_clamp_fusion.1), kind=kCustom, calls=%fused_computation.2.clone | custom fusion | bytes 6291552 | tf_op jit(solution)/shard_map/jit(_take)/gather | solution.py:25
  143.4 6.7 %fusion.4 = (bf16[128,24,512]{2,0,1:T(8,128)(2,1)}, bf16[128,24,512]{2,0,1:T(8,128)(2,1)}) fusion(bf16[24,64,512]{2,1,0:T(8,128)(2,1)S(1)} %copy-done.4, bf16[24,64,512]{2,1,0:T(8,128)(2,1)S(1)} %fusion.33, bf16[24,128,512]{1,2,0:T(8,128)(2,1)} %gather_fusion.2, pred[24]{0:T(512)(128)(4,1)S(1)} %compare_and_fusion, pred[24,64]{1,0:T(8,128)(4,1)S(1)} %iota_compare_fusion), kind=kOutput, calls=%fused_computation.10 | convolution fusion | flops 410910720 | bytes 12584472 | tf_op jit(solution)/shard_map/ctr,trp->ctp/dot_general | solution.py:32
  150.0 4.3 %fusion.10 = f32[8,128,512]{2,0,1:T(8,128)S(1)} fusion(bf16[128,24,512]{2,0,1:T(8,128)(2,1)} %get-tuple-element.16, s32[24]{0:T(128)S(1)} %get-tuple-element.15), kind=kOutput, calls=%fused_computation.22 | convolution fusion | flops 25166016 | bytes 5242976 | tf_op jit(solution)/shard_map/ctp,tb->cbp/dot_general | solution.py:40
  154.3 2.3 %add_convert_fusion = bf16[8,128,512]{2,0,1:T(8,128)(2,1)S(1)} fusion(f32[8,128,512]{2,0,1:T(8,128)S(1)} %fusion.10, bf16[128,24,512]{2,0,1:T(8,128)(2,1)S(1)} %copy-done.2, s32[24]{0:T(128)S(1)} %get-tuple-element.15), kind=kOutput, calls=%fused_computation.38 | convolution fusion | flops 26214592 | bytes 6291552 | tf_op jit(solution)/shard_map/ctp,tb->cbp/dot_general | solution.py:39
  156.6 1.4 copy.57
  158.0 0.0 reduce-scatter.5.cloned.1.call-update
  158.0 0.8 copy.51
  158.8 0.5 copy.49
  159.3 2.0 gather_fusion.3
  161.3 28.8 %reduce-scatter.5.cloned.1.call-done = bf16[128,512]{1,0:T(8,128)(2,1)} async-done(((bf16[128,4096]{1,0:T(8,128)(2,1)}), bf16[128,512]{1,0:T(8,128)(2,1)}) %reduce-scatter.5.cloned.1.call-update) | async-done | bytes 131088 | tf_op jit(solution)/shard_map/reduce_scatter | solution.py:51
  190.1 6.8 %fusion.91 = bf16[16,4,8,128]{3,2,1,0:T(8,128)(2,1)S(1)} fusion(bf16[1,16,512,512]{3,2,1,0:T(8,128)(2,1)} %param.21, bf16[16,128,512]{2,1,0:T(8,128)(2,1)} %gather_fusion.3, pred[16]{0:T(512)(128)(4,1)S(1)} %and_bitcast_fusion, bf16[128,512]{1,0:T(8,128)(2,1)} %reduce-scatter.5.cloned.1.call-done), kind=kOutput, calls=%fused_computation.63 | convolution fusion | flops 1074987008 | bytes 10747920 | tf_op jit(solution)/shard_map/cikq,ikpq->cip/dot_general | solution.py:55
  196.9 0.2 convolution_convert_fusion
  197.1 0.8 copy.52
  (20 shorter events, 0.1 us)
Async XLA Ops:
  7.2 110.6 %copy-start = (bf16[4,128,128]{2,1,0:T(8,128)(2,1)S(1)}, bf16[4,128,128]{2,1,0:T(8,128)(2,1)}, u32[]{:S(2)}) copy-start(bf16[4,128,128]{2,1,0:T(8,128)(2,1)} %param.23) | copy-start | bytes 393220
  7.2 27.8 %all-gather.4.cloned.1.call-start = ((), (), s32[]{:S(2)}) async-start(), calls=%async_computation.2 | async-start | bytes 1179648 | tf_op jit(solution)/shard_map/all_gather | solution.py:46
  8.9 54.4 %all-gather.6.cloned.1.call-start = ((), (), s32[]{:S(2)}) async-start(), calls=%async_computation.3 | async-start | bytes 2359296 | tf_op jit(solution)/shard_map/all_gather | solution.py:84
  9.7 101.2 %reduce-scatter.3.cloned.1.call-start = ((), (), s32[]{:S(2)}) async-start(), calls=%async_computation.4 | async-start | bytes 1179648 | tf_op jit(solution)/shard_map/reduce_scatter | solution.py:51
  9.7 21.0 %collective-permute-start = (bf16[12,64,512]{2,1,0:T(8,128)(2,1)}, bf16[12,64,512]{2,1,0:T(8,128)(2,1)S(1)}, u32[]{:S(2)}, u32[]{:S(2)}) collective-permute-start(bf16[12,64,512]{2,1,0:T(8,128)(2,1)} %param.17), channel_id=1, source_target_pairs={{0,2},{2,0},{1,3},{3,1},{4,6},{6,4},{5,7},{7,5},{8,10},{10,8},{9,1... | collective-permute-start | bytes 2359304 | tf_op jit(solution)/shard_map/ppermute | solution.py:16
  70.6 4.3 %copy-start.3 = (bf16[128,24,512]{2,0,1:T(8,128)(2,1)S(1)}, bf16[128,24,512]{2,0,1:T(8,128)(2,1)}, u32[]{:S(2)}) copy-start(bf16[128,24,512]{2,0,1:T(8,128)(2,1)} %get-tuple-element.19) | copy-start | bytes 9437188
  77.2 1.4 copy-start.6
  78.5 60.8 %all-gather.8.cloned.1.call-start = ((), (), s32[]{:S(2)}) async-start(), calls=%async_computation.5 | async-start | bytes 1179648 | tf_op jit(solution)/shard_map/all_gather | solution.py:46
  118.6 71.5 %reduce-scatter.5.cloned.1.call-start = ((), (), s32[]{:S(2)}) async-start(), calls=%async_computation.6 | async-start | bytes 1179648 | tf_op jit(solution)/shard_map/reduce_scatter | solution.py:51
  139.3 4.0 %copy-start.4 = (bf16[24,64,512]{2,1,0:T(8,128)(2,1)S(1)}, bf16[24,64,512]{2,1,0:T(8,128)(2,1)}, u32[]{:S(2)}) copy-start(bf16[24,64,512]{2,1,0:T(8,128)(2,1)} %all-gather.6.cloned.1.call-done) | copy-start | bytes 4718596
  150.0 4.3 %copy-start.2 = (bf16[128,24,512]{2,0,1:T(8,128)(2,1)S(1)}, bf16[128,24,512]{2,0,1:T(8,128)(2,1)}, u32[]{:S(2)}) copy-start(bf16[128,24,512]{2,0,1:T(8,128)(2,1)} %get-tuple-element.17) | copy-start | bytes 9437188
  156.6 1.4 copy-start.5
  156.6 2.2 %copy-start.1 = (bf16[128,4096]{0,1:T(8,128)(2,1)S(1)}, bf16[128,4096]{0,1:T(8,128)(2,1)}, u32[]{:S(2)}) copy-start(bf16[128,4096]{0,1:T(8,128)(2,1)} %all-gather.8.cloned.1.call-done) | copy-start | bytes 3145732
Sparse Core Ops, SparseCore 0:
  10.2 24.7 all-gather.3
  36.6 26.7 all-gather.5
  78.7 32.2 reduce-scatter.2
  118.8 20.5 all-gather.7
  158.1 31.9 reduce-scatter.4
